TPU v7x, 128 devices: a whole 4x4x4 slice. The times are simulated.
128 devices in a mesh: ctx: 8 (over z, x_hi), fsdp: 16 (over y, x_lo, core).
Axes of the slice: x: 4 (x_hi: 2, x_lo: 2; x = x_hi * 2 + x_lo), y: 4, z: 4, core: 2. Of those that a mesh axis runs over, the one named last changes fastest.
Arguments:
- queries: bfloat16 [16, 2048, 2048], P('fsdp', 'ctx'), may hold values from -36 to 36
- keys: bfloat16 [16, 2048, 512], P('fsdp', 'ctx'), may hold values from -6 to 6
- values: bfloat16 [16, 2048, 512], P('fsdp', 'ctx'), may hold values from -6 to 6
- resid: bfloat16 [16, 2048, 2048], P('fsdp', 'ctx'), may hold values from -6 to 6
- grad_out: bfloat16 [16, 2048, 2048], P('fsdp', 'ctx'), may hold values from -8 to 8
- w_out: bfloat16 [2048, 2048], P(None, 'fsdp'), may hold values from -0.125 to 0.125
- block_list: int32 [16, 8], P('ctx'), may hold values from 0 to 15, as said below
- block_count: int32 [16], P('ctx'), may hold values from 1 to 8, as said below
Outputs:
- mixed: bfloat16 [16, 2048, 2048], P('fsdp', 'ctx')
- query_grad: bfloat16 [16, 2048, 2048], P('fsdp', 'ctx')
- key_grad: bfloat16 [16, 2048, 512], P('fsdp', 'ctx')
- value_grad: bfloat16 [16, 2048, 512], P('fsdp', 'ctx')
- proj_grad: float32 [2048, 2048], P('ctx', 'fsdp')
Inputs may be any that keep to these rules, and one draw needn't show every extreme that they name: `block_list`: row r lists the key blocks of query block r within its sequence: entry 0 is r itself; entries 1 to block_count[r] - 1 are distinct blocks before r; entries from block_count[r] on are ignored and hold r or earlier blocks. block_count[r] is at most min(r + 1, 8); the last query block has exactly 8.
All inputs are finite; a program needn't handle non-finite values.
Results may differ from a plain program's by a relative error of at most 0.025.
Values may be sent and summed in bfloat16 or wider, within the bound.
A program may use at most 192 MiB of HBM per device.

v0:
```python
import math
import jax
import jax.numpy as jnp
from jax import lax
from jax.sharding import PartitionSpec as P

QUERY_HEADS = 16
KEY_VALUE_HEADS = 4
HEAD_DIM = 128
BLOCK_SIZE = 128
KEY_SLOTS = 8


def score_mask(first_row, listed_blocks, live_count):
    query_pos = first_row + jnp.arange(BLOCK_SIZE, dtype=jnp.int32)
    key_pos = listed_blocks[:, None] * BLOCK_SIZE + jnp.arange(BLOCK_SIZE, dtype=jnp.int32)[None, :]
    slot_live = jnp.arange(KEY_SLOTS, dtype=jnp.int32) < live_count
    return (key_pos[None, :, :] <= query_pos[:, None, None]) & slot_live[None, :, None]


def block_weights(query_blk, key_sel, allowed):
    scale = 1.0 / math.sqrt(HEAD_DIM)
    scores = (
        jnp.einsum("qgrd,sbgd->grqsb", query_blk, key_sel, preferred_element_type=jnp.float32)
        * scale
    )
    scores = jnp.where(allowed[None, None], scores, jnp.float32(-1e30))
    top = jnp.max(scores, axis=(3, 4), keepdims=True)
    expon = jnp.exp(scores - top)
    probs = expon / jnp.sum(expon, axis=(3, 4), keepdims=True)
    return (probs, probs.astype(jnp.bfloat16))


def local(queries, keys, values, resid, grad_out, w_out, block_list, block_count):
    scale = 1.0 / math.sqrt(HEAD_DIM)
    query_groups = QUERY_HEADS // KEY_VALUE_HEADS
    seq_rows = queries.shape[1]
    device_local_blocks = seq_rows // BLOCK_SIZE
    first_block = lax.axis_index("ctx") * device_local_blocks
    block_pos = first_block + jnp.arange(device_local_blocks, dtype=jnp.int32)
    complete_keys, complete_values = (
        lax.all_gather(keys, "ctx", axis=1, tiled=True),
        lax.all_gather(values, "ctx", axis=1, tiled=True),
    )
    block_total = complete_keys.shape[1] // BLOCK_SIZE
    blocked_keys = complete_keys[0].reshape(block_total, BLOCK_SIZE, KEY_VALUE_HEADS, HEAD_DIM)
    blocked_values = complete_values[0].reshape(block_total, BLOCK_SIZE, KEY_VALUE_HEADS, HEAD_DIM)
    blocked_queries = queries[0].reshape(
        device_local_blocks, BLOCK_SIZE, KEY_VALUE_HEADS, query_groups, HEAD_DIM
    )

    def forward_block(operands):
        query_blk, listed_blocks, live_count, position = operands
        allowed = score_mask(position * BLOCK_SIZE, listed_blocks, live_count)
        key_sel = jnp.take(blocked_keys, listed_blocks, axis=0)
        value_sel = jnp.take(blocked_values, listed_blocks, axis=0)
        probs, probs_b = block_weights(query_blk, key_sel, allowed)
        attended = jnp.einsum(
            "grqsb,sbgd->qgrd", probs_b, value_sel, preferred_element_type=jnp.float32
        )
        return attended.astype(jnp.bfloat16)

    out_blocks = lax.map(forward_block, (blocked_queries, block_list, block_count, block_pos))
    out_rows = out_blocks.reshape(seq_rows, QUERY_HEADS * HEAD_DIM)
    grad_rows = grad_out[0]
    w_whole = lax.all_gather(w_out, "fsdp", axis=1, tiled=True)
    projected = jnp.dot(out_rows, w_whole, preferred_element_type=jnp.float32)
    attended_gradient = lax.dot_general(
        grad_rows, w_whole, (((1,), (1,)), ((), ())), preferred_element_type=jnp.float32
    )
    mixed = (resid[0].astype(jnp.float32) + projected).astype(jnp.bfloat16)
    output_grad_blocks = attended_gradient.astype(jnp.bfloat16).reshape(
        device_local_blocks, BLOCK_SIZE, KEY_VALUE_HEADS, query_groups, HEAD_DIM
    )

    def backward_block(operands):
        query_blk, out_blk, dout_blk, listed_blocks, live_count, position = operands
        allowed = score_mask(position * BLOCK_SIZE, listed_blocks, live_count)
        key_sel = jnp.take(blocked_keys, listed_blocks, axis=0)
        value_sel = jnp.take(blocked_values, listed_blocks, axis=0)
        probs, probs_b = block_weights(query_blk, key_sel, allowed)
        value_part = jnp.einsum(
            "grqsb,qgrd->sbgd", probs_b, dout_blk, preferred_element_type=jnp.float32
        )
        prob_grads = jnp.einsum(
            "qgrd,sbgd->grqsb", dout_blk, value_sel, preferred_element_type=jnp.float32
        )
        row_dot = jnp.sum(dout_blk.astype(jnp.float32) * out_blk.astype(jnp.float32), axis=-1)
        row_dot = jnp.transpose(row_dot, (1, 2, 0))[:, :, :, None, None]
        score_grads = (probs * (prob_grads - row_dot) * scale).astype(jnp.bfloat16)
        query_part = jnp.einsum(
            "grqsb,sbgd->qgrd", score_grads, key_sel, preferred_element_type=jnp.float32
        ).astype(jnp.bfloat16)
        key_part = jnp.einsum(
            "grqsb,qgrd->sbgd", score_grads, query_blk, preferred_element_type=jnp.float32
        )
        return (query_part, key_part, value_part)

    query_parts, key_fragments, value_fragments = lax.map(
        backward_block,
        (blocked_queries, out_blocks, output_grad_blocks, block_list, block_count, block_pos),
    )
    listed_all = block_list.reshape(-1)
    key_holder = (
        jnp.zeros((block_total, BLOCK_SIZE, KEY_VALUE_HEADS * HEAD_DIM), jnp.float32)
        .at[listed_all]
        .add(
            key_fragments.reshape(
                device_local_blocks * KEY_SLOTS, BLOCK_SIZE, KEY_VALUE_HEADS * HEAD_DIM
            )
        )
    )
    value_holder = (
        jnp.zeros((block_total, BLOCK_SIZE, KEY_VALUE_HEADS * HEAD_DIM), jnp.float32)
        .at[listed_all]
        .add(
            value_fragments.reshape(
                device_local_blocks * KEY_SLOTS, BLOCK_SIZE, KEY_VALUE_HEADS * HEAD_DIM
            )
        )
    )
    key_sum, value_sum = (
        lax.psum_scatter(
            key_holder.reshape(1, block_total * BLOCK_SIZE, KEY_VALUE_HEADS * HEAD_DIM).astype(
                jnp.bfloat16
            ),
            "ctx",
            scatter_dimension=1,
            tiled=True,
        ).astype(jnp.float32),
        lax.psum_scatter(
            value_holder.reshape(1, block_total * BLOCK_SIZE, KEY_VALUE_HEADS * HEAD_DIM).astype(
                jnp.bfloat16
            ),
            "ctx",
            scatter_dimension=1,
            tiled=True,
        ).astype(jnp.float32),
    )
    feature_share = lax.psum_scatter(
        lax.dot_general(
            grad_rows, out_rows, (((0,), (0,)), ((), ())), preferred_element_type=jnp.float32
        ).astype(jnp.bfloat16),
        "fsdp",
        scatter_dimension=0,
        tiled=True,
    )
    proj_grad = (
        lax.psum_scatter(feature_share, "ctx", scatter_dimension=1, tiled=True)
        .astype(jnp.float32)
        .T
    )
    query_grad = query_parts.reshape(1, seq_rows, QUERY_HEADS * HEAD_DIM)
    return (
        mixed[None],
        query_grad,
        key_sum.astype(jnp.bfloat16),
        value_sum.astype(jnp.bfloat16),
        proj_grad,
    )


def solution(mesh):
    in_specs = (
        P("fsdp", "ctx", None),
        P("fsdp", "ctx", None),
        P("fsdp", "ctx", None),
        P("fsdp", "ctx", None),
        P("fsdp", "ctx", None),
        P(None, "fsdp"),
        P("ctx", None),
        P("ctx"),
    )
    out_specs = (
        P("fsdp", "ctx", None),
        P("fsdp", "ctx", None),
        P("fsdp", "ctx", None),
        P("fsdp", "ctx", None),
        P("ctx", "fsdp"),
    )
    return jax.shard_map(local, mesh=mesh, in_specs=in_specs, out_specs=out_specs, check_vma=False)
```

profile of v0, /device:TPU:0, one launch (start us, length us, event | category | flops | bytes accessed | tf_op | source)
XLA Modules:
  0.0 542.2 jit_solution(563951076636998370)
XLA Ops:
  12.5 54.5 %all-gather.4.cloned.1.call-done = bf16[1,2048,512]{2,1,0:T(8,128)(2,1)} async-done(((bf16[1,256,512]{2,1,0:T(8,128)(2,1)}), bf16[1,2048,512]{2,1,0:T(8,128)(2,1)}) %all-gather.4.cloned.1.call-update) | async-done | bytes 2097168 | tf_op jit(solution)/shard_map/all_gather | solution.py:43
  67.0 4.0 reshape_squeeze.9
  71.0 50.3 %all-gather.6.cloned.1.call-done = bf16[1,2048,512]{2,1,0:T(8,128)(2,1)} async-done(((bf16[1,256,512]{2,1,0:T(8,128)(2,1)}), bf16[1,2048,512]{2,1,0:T(8,128)(2,1)}) %all-gather.6.cloned.1.call-update) | async-done | bytes 2097168 | tf_op jit(solution)/shard_map/all_gather | solution.py:42
  121.3 4.0 reshape_squeeze.10
  125.3 35.7 %while.24 = (s32[]{:T(128)}, bf16[2,128,4,4,128]{1,4,3,2,0:T(8,128)(2,1)}, s32[2,8]{1,0:T(2,128)S(1)}, bf16[16,128,4,128]{3,2,1,0:T(4,128)(2,1)}, s32[2]{0:T(128...) while((s32[]{:T(128)}, ...), condition=%wide.region_3.5_spmd, body=%wide.region_0.4_spmd.sunk | while | flops 1100478720 | bytes 45667840 | solution.py:63
  125.3 3.0 gather_fusion
  128.4 3.0 gather_fusion.1
  143.1 3.0 gather_fusion
  146.1 3.2 gather_fusion.1
  163.9 5.6 %convert_bitcast_fusion = bf16[2048,2048]{0,1:T(8,128)(2,1)} fusion(bf16[256,2048]{1,0:T(8,128)(2,1)S(1)} %reshape.176, bf16[1,256,2048]{2,1,0:T(8,128)(2,1)S(1)} %copy-done), kind=kOutput, calls=%fused_computation.87 | convolution fusion | flops 2151677952 | bytes 10485760 | tf_op jit(solution)/shard_map/dot_general | solution.py:141
  169.5 12.3 %copy.122 = bf16[2048,2048]{1,0:T(8,128)(2,1)} copy(bf16[2048,2048]{0,1:T(8,128)(2,1)} %convert_bitcast_fusion) | data formatting | bytes 16777216
  182.6 5.7 %convolution_convert_fusion = bf16[256,2048]{1,0:T(8,128)(2,1)S(1)} fusion(bf16[2048,2048]{1,0:T(8,128)(2,1)} %all-gather.8.cloned.1.call-done, bf16[1,256,2048]{2,1,0:T(8,128)(2,1)S(1)} %copy-done), kind=kOutput, calls=%fused_computation.90 | convolution fusion | flops 2148007936 | bytes 10485760 | tf_op jit(solution)/shard_map/dot_general | solution.py:68
  189.9 91.2 %reduce-scatter.13.cloned.1.call-done = bf16[128,2048]{1,0:T(8,128)(2,1)} async-done(((bf16[2048,2048]{1,0:T(8,128)(2,1)}), bf16[128,2048]{1,0:T(8,128)(2,1)}) %reduce-scatter.13.cloned.1.call-update) | async-done | bytes 524304
  283.2 78.1 %while.25 = (s32[]{:T(128)}, bf16[2,128,4,4,128]{4,3,2,1,0:T(4,128)(2,1)}, f32[2,8,128,4,128]{2,4,3,1,0:T(8,128)}, f32[2,8,128,4,128]{2,4,3,1,0:T(8,128)}, s32[2...) while((s32[]{:T(128)}, ...), condition=%wide.region_8.10_spmd, body=%wide.region_4.9_spmd.sunk | while | flops 2728915200 | bytes 224614144 | solution.py:99
  283.2 3.0 gather_fusion.2
  286.3 3.0 gather_fusion.3
  297.9 2.6 fusion.107
  302.3 3.4 fusion.109
  310.0 5.0 fusion.111
  322.3 3.0 gather_fusion.2
  325.4 3.0 gather_fusion.3
  341.4 3.4 fusion.109
  349.1 5.0 fusion.111
  361.3 5.4 copy.85
  369.2 9.4 %scatter_fusion = f32[16,128,512]{2,1,0:T(8,128)} fusion(f32[16,128,512]{2,1,0:T(8,128)} %broadcast.137.clone, s32[16]{0:T(128)S(1)} %copy-done.17, f32[16,128,512]{2,1,0:T(8,128)} %copy.85), kind=kCustom, calls=%fused_computation.4 | custom fusion | flops 1048576 | bytes 12582976 | tf_op jit(solution)/shard_map/scatter-add | solution.py:107
  378.6 3.8 convert_element_type.85
  382.5 5.4 copy.87
  390.3 9.4 %scatter_fusion.1 = f32[16,128,512]{2,1,0:T(8,128)} fusion(f32[16,128,512]{2,1,0:T(8,128)} %broadcast.137.clone.1, s32[16]{0:T(128)S(1)} %copy-done.17, f32[16,128,512]{2,1,0:T(8,128)} %copy.87), kind=kCustom, calls=%fused_computation.5 | custom fusion | flops 1048576 | bytes 12582976 | tf_op jit(solution)/shard_map/scatter-add | solution.py:116
  399.8 4.0 convert_element_type.87
  405.4 7.0 %fusion.64 = bf16[1,256,2048]{2,1,0:T(8,128)(2,1)} fusion(bf16[256,2048]{1,0:T(8,128)(2,1)S(1)} %copy-done.10, bf16[2048,2048]{1,0:T(8,128)(2,1)} %all-gather.8.cloned.1.call-done, bf16[1,256,2048]{2,1,0:T(8,128)(2,1)} %param.17), kind=kOutput, calls=%fused_computation.91 | convolution fusion | flops 2149056512 | bytes 11534336 | tf_op jit(solution)/shard_map/dot_general | solution.py:67
  413.9 42.8 %reduce-scatter.7.cloned.1.call-done = bf16[1,256,512]{2,1,0:T(8,128)(2,1)} async-done(((bf16[1,2048,512]{2,1,0:T(8,128)(2,1)}), bf16[1,256,512]{2,1,0:T(8,128)(2,1)}) %reduce-scatter.7.cloned.1.call-update) | async-done | bytes 262160 | tf_op jit(solution)/shard_map/reduce_scatter | solution.py:123
  456.7 78.6 %reduce-scatter.9.cloned.1.call-done = bf16[1,256,512]{2,1,0:T(8,128)(2,1)} async-done(((bf16[1,2048,512]{2,1,0:T(8,128)(2,1)}), bf16[1,256,512]{2,1,0:T(8,128)(2,1)}) %reduce-scatter.9.cloned.1.call-update) | async-done | bytes 262160 | tf_op jit(solution)/shard_map/reduce_scatter | solution.py:131
  (162 shorter events, 87.4 us)
Async XLA Ops:
  7.2 156.7 %copy-start = (bf16[1,256,2048]{2,1,0:T(8,128)(2,1)S(1)}, bf16[1,256,2048]{2,1,0:T(8,128)(2,1)}, u32[]{:S(2)}) copy-start(bf16[1,256,2048]{2,1,0:T(8,128)(2,1)} %param.18) | copy-start | bytes 3145732
  7.2 118.1 %copy-start.16 = (s32[2,8]{1,0:T(2,128)S(1)}, s32[2,8]{1,0:T(2,128)}, u32[]{:S(2)}) copy-start(s32[2,8]{1,0:T(2,128)} %param.20) | copy-start | bytes 196
  7.2 118.1 %copy-start.18 = (s32[2]{0:T(128)S(1)}, s32[2]{0:T(128)}, u32[]{:S(2)}) copy-start(s32[2]{0:T(128)} %param.21) | copy-start | bytes 28
  7.2 59.8 %all-gather.4.cloned.1.call-start = ((), (), s32[]{:S(2)}) async-start(), calls=%async_computation.4 | async-start | bytes 2359296 | tf_op jit(solution)/shard_map/all_gather | solution.py:43
  7.9 113.4 %all-gather.6.cloned.1.call-start = ((), (), s32[]{:S(2)}) async-start(), calls=%async_computation.5 | async-start | bytes 2359296 | tf_op jit(solution)/shard_map/all_gather | solution.py:42
  8.7 173.9 %all-gather.8.cloned.1.call-start = ((), (), s32[]{:S(2)}) async-start(), calls=%async_computation.6 | async-start | bytes 8912896 | tf_op jit(solution)/shard_map/all_gather | solution.py:66
  9.4 271.6 %reduce-scatter.13.cloned.1.call-start = ((), (), s32[]{:S(2)}) async-start(), calls=%async_computation.10 | async-start | bytes 8912896
  135.2 4.3 copy-start.7
  153.1 4.3 copy-start.7
  163.9 18.0 %copy-start.9 = (bf16[256,2048]{1,0:T(8,128)(2,1)}, bf16[256,2048]{1,0:T(8,128)(2,1)S(1)}, u32[]{:S(2)}) copy-start(bf16[256,2048]{1,0:T(8,128)(2,1)S(1)} %reshape.176) | copy-start | bytes 3145732
  181.9 230.5 %reduce-scatter.11.cloned.1.call-start = ((), (), s32[]{:S(2)}) async-start(), calls=%async_computation.9 | async-start | bytes 589824 | tf_op jit(solution)/shard_map/reduce_scatter | solution.py:149
  283.1 173.6 %reduce-scatter.7.cloned.1.call-start = ((), (), s32[]{:S(2)}) async-start(), calls=%async_computation.7 | async-start | bytes 2359296 | tf_op jit(solution)/shard_map/reduce_scatter | solution.py:123
  297.9 4.4 copy-start.6
  300.6 5.2 copy-start.2
  305.7 2.0 copy-start.3
  310.0 5.0 copy-start.4
  310.0 5.0 copy-start.5
  314.9 2.2 copy-start.11
  314.9 3.5 copy-start.13
  319.0 3.2 copy-start.14
  337.0 4.4 copy-start.6
  339.6 5.2 copy-start.2
  349.1 5.0 copy-start.4
  349.1 5.0 copy-start.5
  354.0 2.2 copy-start.11
  354.0 3.4 copy-start.13
  358.1 3.2 copy-start.14
  361.3 7.9 %copy-start.17 = (s32[16]{0:T(128)S(1)}, s32[16]{0:T(128)}, u32[]{:S(2)}) copy-start(s32[16]{0:T(128)} %fusion.67) | copy-start | bytes 196
  382.4 152.9 %reduce-scatter.9.cloned.1.call-start = ((), (), s32[]{:S(2)}) async-start(), calls=%async_computation.8 | async-start | bytes 2359296 | tf_op jit(solution)/shard_map/reduce_scatter | solution.py:131
  390.3 13.4 %copy-start.15 = (bf16[2,128,4,4,128]{4,3,2,1,0:T(4,128)(2,1)S(1)}, bf16[2,128,4,4,128]{4,3,2,1,0:T(4,128)(2,1)}, u32[]{:S(2)}) copy-start(bf16[2,128,4,4,128]{4,3,2,1,0:T(4,128)(2,1)} %get-tuple-element.113) | copy-start | bytes 3145732
  399.7 5.6 %copy-start.10 = (bf16[256,2048]{1,0:T(8,128)(2,1)S(1)}, bf16[256,2048]{1,0:T(8,128)(2,1)}, u32[]{:S(2)}) copy-start(bf16[256,2048]{1,0:T(8,128)(2,1)} %copy-done.9) | copy-start | bytes 3145732
  403.7 131.6 %copy-start.1 = (bf16[1,256,2048]{2,1,0:T(8,128)(2,1)S(1)}, bf16[1,256,2048]{2,1,0:T(8,128)(2,1)}, u32[]{:S(2)}) copy-start(bf16[1,256,2048]{2,1,0:T(8,128)(2,1)} %param.18) | copy-start | bytes 3145732
  (5 other events, 7.9 us)
Sparse Core Ops, SparseCore 0:
  10.4 56.5 all-gather.3
  69.4 51.8 all-gather.5
  123.0 58.0 all-gather.7
  183.3 97.6 reduce-scatter.12
  284.4 69.2 reduce-scatter.10
  382.6 74.0 reduce-scatter.6
  461.4 73.8 reduce-scatter.8
where the time goes:
time: 544 us; the launch traced here: 542 us
  waiting for transfers between devices  320 us (59%)
  local copies, waits for them, and re-layouts  103 us (19%)
  matrix products  55.3 us (10%)
  other arithmetic  46.2 us (8%)
  between operations  14.3 us (3%)
    unnamed x8, waiting for transfers between devices  93.3 us
    reduce_scatter x1, waiting for transfers between devices, local(): lax.psum_scatter(value_holder.reshape(1, block_total * BLOCK_SIZE, KEY_VA...  78.6 us
    all_gather x1, waiting for transfers between devices, local(): lax.all_gather(values, 'ctx', axis=1, tiled=True)  54.5 us
    all_gather x1, waiting for transfers between devices, local(): lax.all_gather(keys, 'ctx', axis=1, tiled=True)  50.3 us
    reduce_scatter x1, waiting for transfers between devices, local(): lax.psum_scatter(key_holder.reshape(1, block_total * BLOCK_SIZE, KEY_VALU...  42.8 us
    while x44, local copies, waits for them, and re-layouts  16.2 us
    unnamed x18, local copies, waits for them, and re-layouts  14.4 us
  transfers between devices with their start and end apart: 7, of which 5 were waited for; matrix products, arithmetic and copies ran while one was open for 34% of the time, Pallas kernels for 0%

commit v1 on v0

--- a/solution.py
+++ b/solution.py
@@ -9,6 +9,16 @@
 HEAD_DIM = 128
 BLOCK_SIZE = 128
 KEY_SLOTS = 8
+
+
+def step_on_members_all(my_data):
+    placed = jnp.concatenate(
+        lax.all_to_all(
+            jnp.stack(tuple((my_data for _ in range(lax.axis_size("ctx")))), 0), "ctx", 0, 0
+        ),
+        1,
+    )
+    return placed
 
 
 def score_mask(first_row, listed_blocks, live_count):
@@ -40,7 +50,7 @@
     block_pos = first_block + jnp.arange(device_local_blocks, dtype=jnp.int32)
     complete_keys, complete_values = (
         lax.all_gather(keys, "ctx", axis=1, tiled=True),
-        lax.all_gather(values, "ctx", axis=1, tiled=True),
+        step_on_members_all(values),
     )
     block_total = complete_keys.shape[1] // BLOCK_SIZE
     blocked_keys = complete_keys[0].reshape(block_total, BLOCK_SIZE, KEY_VALUE_HEADS, HEAD_DIM)

time: 544 us -> 501 us (0.921)
  waiting for transfers between devices: 320 us -> 267 us
  starting transfers between devices: 0.28 us -> 8.41 us
    all_gather x1 -> x0, waiting for transfers between devices: 54.5 us -> none  [local(): lax.all_gather(values, 'ctx', axis=1, tiled=True)]
    all_to_all x0 -> x1, waiting for transfers between devices: none -> 26.1 us  [step_on_members_all(): lax.all_to_all(jnp.stack(tuple((my_data for _ in range(lax.axis_size('ctx...]
    all_gather x1, waiting for transfers between devices: 50.3 us -> 26.7 us  [local(): lax.all_gather(keys, 'ctx', axis=1, tiled=True)]
    all_to_all x0 -> x1, starting transfers between devices: none -> 7.99 us  [step_on_members_all(): lax.all_to_all(jnp.stack(tuple((my_data for _ in range(lax.axis_size('ctx...]
    unnamed x8 -> x7, waiting for transfers between devices: 93.3 us -> 92.5 us
  transfers between devices with their start and end apart: 7 -> 7, of which waited for: 5 -> 5; matrix products, arithmetic and copies ran while one was open for 34% -> 38% of each run, Pallas kernels for 0% -> 0%
where the time goes in v1:
time: 501 us; the launch traced here: 500 us
  waiting for transfers between devices  267 us (53%)
  local copies, waits for them, and re-layouts  106 us (21%)
  matrix products  55.3 us (11%)
  other arithmetic  45.8 us (9%)
  between operations  14.2 us (3%)
  starting transfers between devices  8.41 us (2%)
    unnamed x7, waiting for transfers between devices  92.5 us
    reduce_scatter x1, waiting for transfers between devices, local(): lax.psum_scatter(value_holder.reshape(1, block_total * BLOCK_SIZE, KEY_VA...  78.5 us
    reduce_scatter x1, waiting for transfers between devices, local(): lax.psum_scatter(key_holder.reshape(1, block_total * BLOCK_SIZE, KEY_VALU...  43.2 us
    all_gather x1, waiting for transfers between devices, local(): lax.all_gather(keys, 'ctx', axis=1, tiled=True)  26.7 us
    all_to_all x1, waiting for transfers between devices, step_on_members_all(): lax.all_to_all(jnp.stack(tuple((my_data for _ in range(lax.axis_size('ctx...  26.1 us
    while x44, local copies, waits for them, and re-layouts  16.1 us
    unnamed x18, local copies, waits for them, and re-layouts  14.6 us
    dot_general x4, matrix products, block_weights(): jnp.einsum('qgrd,sbgd->grqsb', query_blk, key_sel, preferred_element_type...  10.3 us
  transfers between devices with their start and end apart: 7, of which 5 were waited for; matrix products, arithmetic and copies ran while one was open for 38% of the time, Pallas kernels for 0%

profile of v1, /device:TPU:0, one launch (start us, length us, event | category | flops | bytes accessed | tf_op | source)
XLA Modules:
  0.0 499.9 jit_solution(9950152109460023355)
XLA Ops:
  11.1 8.0 %all-to-all-start = ((bf16[8,1,256,512]{3,2,1,0:T(8,128)(2,1)}), bf16[8,1,256,512]{3,2,1,0:T(8,128)(2,1)S(1)}, u32[]{:S(2)}, u32[]{:S(2)}) async-start(bf16[8,1,256,512]{3,2,1,0:T(8,128)(2,1)} %stack.2), calls=%async_computation | async-start | bytes 4194304 | tf_op jit(solution)/shard_map/all_to_all | solution.py:16
  24.3 26.1 %all-to-all-done = bf16[8,1,256,512]{3,2,1,0:T(8,128)(2,1)S(1)} async-done(((bf16[8,1,256,512]{3,2,1,0:T(8,128)(2,1)}), bf16[8,1,256,512]{3,2,1,0:T(8,128)(2,1)S(1)}, u32[]{:S(2)}, u32[]{:S(2)}) %all-to-all-start) | async-done | bytes 2097184 | tf_op jit(solution)/shard_map/all_to_all | solution.py:16
  52.5 26.7 %all-gather.3.cloned.1.call-done = bf16[1,2048,512]{2,1,0:T(8,128)(2,1)} async-done(((bf16[1,256,512]{2,1,0:T(8,128)(2,1)}), bf16[1,2048,512]{2,1,0:T(8,128)(2,1)}) %all-gather.3.cloned.1.call-update) | async-done | bytes 2097168 | tf_op jit(solution)/shard_map/all_gather | solution.py:52
  79.2 4.0 reshape_squeeze.6
  83.1 35.7 %while.24 = (s32[]{:T(128)}, bf16[2,128,4,4,128]{1,4,3,2,0:T(8,128)(2,1)}, s32[2,8]{1,0:T(2,128)S(1)}, bf16[16,128,4,128]{3,2,1,0:T(4,128)(2,1)}, s32[2]{0:T(128...) while((s32[]{:T(128)}, ...), condition=%wide.region_3.5_spmd, body=%wide.region_0.4_spmd.sunk | while | flops 1100478720 | bytes 45667840 | solution.py:73
  83.2 3.0 gather_fusion
  86.2 3.0 gather_fusion.1
  100.9 3.0 gather_fusion
  104.0 3.2 gather_fusion.1
  121.7 5.6 %convert_bitcast_fusion = bf16[2048,2048]{0,1:T(8,128)(2,1)} fusion(bf16[256,2048]{1,0:T(8,128)(2,1)S(1)} %reshape.179, bf16[1,256,2048]{2,1,0:T(8,128)(2,1)S(1)} %copy-done), kind=kOutput, calls=%fused_computation.87 | convolution fusion | flops 2151677952 | bytes 10485760 | tf_op jit(solution)/shard_map/dot_general | solution.py:151
  127.3 12.5 %copy.122 = bf16[2048,2048]{1,0:T(8,128)(2,1)} copy(bf16[2048,2048]{0,1:T(8,128)(2,1)} %convert_bitcast_fusion) | data formatting | bytes 16777216
  140.7 5.7 %convolution_convert_fusion = bf16[256,2048]{1,0:T(8,128)(2,1)S(1)} fusion(bf16[2048,2048]{1,0:T(8,128)(2,1)} %all-gather.5.cloned.1.call-done, bf16[1,256,2048]{2,1,0:T(8,128)(2,1)S(1)} %copy-done), kind=kOutput, calls=%fused_computation.90 | convolution fusion | flops 2148007936 | bytes 10485760 | tf_op jit(solution)/shard_map/dot_general | solution.py:78
  148.0 91.0 %reduce-scatter.13.cloned.1.call-done = bf16[128,2048]{1,0:T(8,128)(2,1)} async-done(((bf16[2048,2048]{1,0:T(8,128)(2,1)}), bf16[128,2048]{1,0:T(8,128)(2,1)}) %reduce-scatter.13.cloned.1.call-update) | async-done | bytes 524304
  241.2 78.1 %while.25 = (s32[]{:T(128)}, bf16[2,128,4,4,128]{4,3,2,1,0:T(4,128)(2,1)}, f32[2,8,128,4,128]{2,4,3,1,0:T(8,128)}, f32[2,8,128,4,128]{2,4,3,1,0:T(8,128)}, s32[2...) while((s32[]{:T(128)}, ...), condition=%wide.region_8.10_spmd, body=%wide.region_4.9_spmd.sunk | while | flops 2728915200 | bytes 224614144 | solution.py:109
  241.2 3.0 gather_fusion.2
  244.2 3.0 gather_fusion.3
  255.9 2.6 fusion.107
  260.3 3.4 fusion.109
  267.9 5.0 fusion.111
  280.3 3.0 gather_fusion.2
  283.3 3.0 gather_fusion.3
  299.4 3.4 fusion.109
  307.0 5.0 fusion.111
  319.2 5.4 %copy.85 = f32[16,128,512]{2,1,0:T(8,128)} copy(f32[16,128,512]{1,2,0:T(8,128)} %bitcast.240) | data formatting | bytes 8388608 | tf_op jit(solution)/shard_map/reshape | solution.py:118
  327.1 9.2 %scatter_fusion = f32[16,128,512]{2,1,0:T(8,128)} fusion(f32[16,128,512]{2,1,0:T(8,128)} %broadcast.140.clone, s32[16]{0:T(128)S(1)} %copy-done.17, f32[16,128,512]{2,1,0:T(8,128)} %copy.85), kind=kCustom, calls=%fused_computation.4 | custom fusion | flops 1048576 | bytes 12582976 | tf_op jit(solution)/shard_map/scatter-add | solution.py:117
  336.3 3.8 convert_element_type.85
  340.2 5.4 %copy.87 = f32[16,128,512]{2,1,0:T(8,128)} copy(f32[16,128,512]{1,2,0:T(8,128)} %bitcast.241) | data formatting | bytes 8388608 | tf_op jit(solution)/shard_map/reshape | solution.py:127
  348.0 9.2 %scatter_fusion.1 = f32[16,128,512]{2,1,0:T(8,128)} fusion(f32[16,128,512]{2,1,0:T(8,128)} %broadcast.140.clone.1, s32[16]{0:T(128)S(1)} %copy-done.17, f32[16,128,512]{2,1,0:T(8,128)} %copy.87), kind=kCustom, calls=%fused_computation.5 | custom fusion | flops 1048576 | bytes 12582976 | tf_op jit(solution)/shard_map/scatter-add | solution.py:126
  357.3 4.0 convert_element_type.87
  362.9 7.0 %fusion.64 = bf16[1,256,2048]{2,1,0:T(8,128)(2,1)} fusion(bf16[256,2048]{1,0:T(8,128)(2,1)S(1)} %copy-done.10, bf16[2048,2048]{1,0:T(8,128)(2,1)} %all-gather.5.cloned.1.call-done, bf16[1,256,2048]{2,1,0:T(8,128)(2,1)} %param.17), kind=kOutput, calls=%fused_computation.91 | convolution fusion | flops 2149056512 | bytes 11534336 | tf_op jit(solution)/shard_map/dot_general | solution.py:77
  371.4 43.2 %reduce-scatter.7.cloned.1.call-done = bf16[1,256,512]{2,1,0:T(8,128)(2,1)} async-done(((bf16[1,2048,512]{2,1,0:T(8,128)(2,1)}), bf16[1,256,512]{2,1,0:T(8,128)(2,1)}) %reduce-scatter.7.cloned.1.call-update) | async-done | bytes 262160 | tf_op jit(solution)/shard_map/reduce_scatter | solution.py:133
  414.6 78.5 %reduce-scatter.9.cloned.1.call-done = bf16[1,256,512]{2,1,0:T(8,128)(2,1)} async-done(((bf16[1,2048,512]{2,1,0:T(8,128)(2,1)}), bf16[1,256,512]{2,1,0:T(8,128)(2,1)}) %reduce-scatter.9.cloned.1.call-update) | async-done | bytes 262160 | tf_op jit(solution)/shard_map/reduce_scatter | solution.py:141
  (162 shorter events, 93.3 us)
Async XLA Ops:
  7.2 114.6 %copy-start = (bf16[1,256,2048]{2,1,0:T(8,128)(2,1)S(1)}, bf16[1,256,2048]{2,1,0:T(8,128)(2,1)}, u32[]{:S(2)}) copy-start(bf16[1,256,2048]{2,1,0:T(8,128)(2,1)} %param.18) | copy-start | bytes 3145732
  7.2 72.0 %all-gather.3.cloned.1.call-start = ((), (), s32[]{:S(2)}) async-start(), calls=%async_computation.5 | async-start | bytes 2359296 | tf_op jit(solution)/shard_map/all_gather | solution.py:52
  7.9 132.8 %all-gather.5.cloned.1.call-start = ((), (), s32[]{:S(2)}) async-start(), calls=%async_computation.6 | async-start | bytes 8912896 | tf_op jit(solution)/shard_map/all_gather | solution.py:76
  11.1 72.0 %copy-start.16 = (s32[2,8]{1,0:T(2,128)S(1)}, s32[2,8]{1,0:T(2,128)}, u32[]{:S(2)}) copy-start(s32[2,8]{1,0:T(2,128)} %param.20) | copy-start | bytes 196
  11.1 72.0 %copy-start.18 = (s32[2]{0:T(128)S(1)}, s32[2]{0:T(128)}, u32[]{:S(2)}) copy-start(s32[2]{0:T(128)} %param.21) | copy-start | bytes 28
  11.1 39.3 %all-to-all-start = ((bf16[8,1,256,512]{3,2,1,0:T(8,128)(2,1)}), bf16[8,1,256,512]{3,2,1,0:T(8,128)(2,1)S(1)}, u32[]{:S(2)}, u32[]{:S(2)}) async-start(bf16[8,1,256,512]{3,2,1,0:T(8,128)(2,1)} %stack.2), calls=%async_computation | async-start | bytes 4194304 | tf_op jit(solution)/shard_map/all_to_all | solution.py:16
  19.1 219.9 %reduce-scatter.13.cloned.1.call-start = ((), (), s32[]{:S(2)}) async-start(), calls=%async_computation.10 | async-start | bytes 8912896
  93.0 4.3 copy-start.7
  111.0 4.3 copy-start.7
  121.7 18.1 %copy-start.9 = (bf16[256,2048]{1,0:T(8,128)(2,1)}, bf16[256,2048]{1,0:T(8,128)(2,1)S(1)}, u32[]{:S(2)}) copy-start(bf16[256,2048]{1,0:T(8,128)(2,1)S(1)} %reshape.179) | copy-start | bytes 3145732
  139.8 230.1 %reduce-scatter.11.cloned.1.call-start = ((), (), s32[]{:S(2)}) async-start(), calls=%async_computation.9 | async-start | bytes 589824 | tf_op jit(solution)/shard_map/reduce_scatter | solution.py:159
  241.1 173.5 %reduce-scatter.7.cloned.1.call-start = ((), (), s32[]{:S(2)}) async-start(), calls=%async_computation.7 | async-start | bytes 2359296 | tf_op jit(solution)/shard_map/reduce_scatter | solution.py:133
  255.9 4.4 copy-start.6
  258.5 5.2 %copy-start.2 = (f32[4,8,128,128,4]{3,2,4,1,0:T(8,128)}, f32[4,8,128,128,4]{3,2,4,1,0:T(8,128)S(1)}, u32[]{:S(2)}) copy-start(f32[4,8,128,128,4]{3,2,4,1,0:T(8,128)S(1)} %get-tuple-element.387) | copy-start | bytes 25165828 | tf_op jit(solution)/shard_map/while
  263.7 2.0 copy-start.3
  267.9 5.0 copy-start.4
  267.9 5.0 %copy-start.5 = (bf16[2,128,4,4,128]{4,1,3,2,0:T(8,128)(2,1)S(1)}, bf16[2,128,4,4,128]{4,1,3,2,0:T(8,128)(2,1)}, u32[]{:S(2)}) copy-start(bf16[2,128,4,4,128]{4,1,3,2,0:T(8,128)(2,1)} %get-tuple-element.458) | copy-start | bytes 3145732 | tf_op jit(solution)/shard_map/while
  272.9 2.2 copy-start.11
  272.9 3.5 copy-start.13
  277.0 3.2 copy-start.14
  295.0 4.4 copy-start.6
  297.6 5.2 %copy-start.2 = (f32[4,8,128,128,4]{3,2,4,1,0:T(8,128)}, f32[4,8,128,128,4]{3,2,4,1,0:T(8,128)S(1)}, u32[]{:S(2)}) copy-start(f32[4,8,128,128,4]{3,2,4,1,0:T(8,128)S(1)} %get-tuple-element.387) | copy-start | bytes 25165828 | tf_op jit(solution)/shard_map/while
  307.0 5.0 %copy-start.4 = (bf16[4,4,128,8,128]{2,4,1,3,0:T(8,128)(2,1)S(1)}, bf16[4,4,128,8,128]{2,4,1,3,0:T(8,128)(2,1)}, u32[]{:S(2)}) copy-start(bf16[4,4,128,8,128]{2,4,1,3,0:T(8,128)(2,1)} %copy-done.3) | copy-start | bytes 12582916 | tf_op jit(solution)/shard_map/while
  307.0 5.0 %copy-start.5 = (bf16[2,128,4,4,128]{4,1,3,2,0:T(8,128)(2,1)S(1)}, bf16[2,128,4,4,128]{4,1,3,2,0:T(8,128)(2,1)}, u32[]{:S(2)}) copy-start(bf16[2,128,4,4,128]{4,1,3,2,0:T(8,128)(2,1)} %get-tuple-element.458) | copy-start | bytes 3145732 | tf_op jit(solution)/shard_map/while
  312.0 2.2 copy-start.11
  312.0 3.4 copy-start.13
  316.0 3.2 copy-start.14
  319.2 7.8 %copy-start.17 = (s32[16]{0:T(128)S(1)}, s32[16]{0:T(128)}, u32[]{:S(2)}) copy-start(s32[16]{0:T(128)} %fusion.67) | copy-start | bytes 196
  340.2 152.9 %reduce-scatter.9.cloned.1.call-start = ((), (), s32[]{:S(2)}) async-start(), calls=%async_computation.8 | async-start | bytes 2359296 | tf_op jit(solution)/shard_map/reduce_scatter | solution.py:141
  348.0 13.2 %copy-start.15 = (bf16[2,128,4,4,128]{4,3,2,1,0:T(4,128)(2,1)S(1)}, bf16[2,128,4,4,128]{4,3,2,1,0:T(4,128)(2,1)}, u32[]{:S(2)}) copy-start(bf16[2,128,4,4,128]{4,3,2,1,0:T(4,128)(2,1)} %get-tuple-element.113) | copy-start | bytes 3145732
  357.3 5.6 %copy-start.10 = (bf16[256,2048]{1,0:T(8,128)(2,1)S(1)}, bf16[256,2048]{1,0:T(8,128)(2,1)}, u32[]{:S(2)}) copy-start(bf16[256,2048]{1,0:T(8,128)(2,1)} %copy-done.9) | copy-start | bytes 3145732
  361.3 131.8 %copy-start.1 = (bf16[1,256,2048]{2,1,0:T(8,128)(2,1)S(1)}, bf16[1,256,2048]{2,1,0:T(8,128)(2,1)}, u32[]{:S(2)}) copy-start(bf16[1,256,2048]{2,1,0:T(8,128)(2,1)} %param.18) | copy-start | bytes 3145732
  (5 other events, 7.8 us)
Sparse Core Ops, SparseCore 0:
  10.4 68.7 all-gather.2
  80.8 58.2 all-gather.4
  141.5 97.4 reduce-scatter.12
  242.4 69.3 reduce-scatter.10
  340.3 74.2 reduce-scatter.6
  419.2 73.8 reduce-scatter.8
